TPU v7x, 32 devices: a whole 2x2x4 slice. The times are simulated.
32 devices in a mesh: section: 4 (over z), expert: 8 (over y, x, core).
Axes of the slice: x: 2, y: 2, z: 4, core: 2. Of those that a mesh axis runs over, the one named last changes fastest.
Arguments:
- hidden_fwd: bfloat16 [4, 2048, 1536], P('section', 'expert'), may hold values from -6 to 6
- down_weight: bfloat16 [8, 1536, 2048], P('expert'), may hold values from -0.15625 to 0.15625
- residual: bfloat16 [4, 256, 2048], P('section', 'expert'), may hold values from -6 to 6
- route_fwd: int32 [4, 256, 8], P('section', 'expert'), may hold values from 0 to 255, as said below
- gate_fwd: float32 [4, 256, 8], P('section', 'expert'), may hold values from 0.05 to 0.35
- hidden_bwd: bfloat16 [4, 2048, 1536], P('section', 'expert'), may hold values from -0.59765625 to 0.59765625
- route_bwd: int32 [4, 256, 8], P('section', 'expert'), may hold values from 0 to 255, as said below
- gate_bwd: float32 [4, 256, 8], P('section', 'expert'), may hold values from 0.05 to 0.35
- upstream: bfloat16 [4, 256, 2048], P('section', 'expert'), may hold values from -3 to 3
Outputs:
- next_input: bfloat16 [4, 256, 2048], P('section', 'expert')
- hidden_grad: bfloat16 [4, 2048, 1536], P('section', 'expert')
- gate_grad: float32 [4, 2048], P('section', 'expert')
Inputs may be any that keep to these rules, and one draw needn't show every extreme that they name: `route_fwd`: for each section, the 256 entries of the tokens of one device are all different; entry // 32 names the expert and entry % 32 a position among that device's rows for it, so every expert receives exactly 32 routes from each device on each section; the 8 entries of a token name different experts. `route_bwd`: same law as route_fwd, drawn independently.
All inputs are finite; a program needn't handle non-finite values.
Results may differ from a plain program's by a relative error of at most 0.0051.
Values may be sent and summed in bfloat16 or wider, within the bound.
A program may use at most 64 MiB of HBM per device.

v0:
```python
import jax
import jax.numpy as jnp
from jax import lax
from jax.sharding import PartitionSpec as P

TOP = 8


def from_behind(block, axis, distance):
    devices = range(lax.axis_size(axis))
    route = [((i - distance) % len(devices), i) for i in devices]
    return lax.ppermute(block, axis, route)


def forward_local(hidden_fwd, down_weight):
    return jnp.dot(hidden_fwd[0], down_weight[0], preferred_element_type=jnp.float32).astype(
        jnp.bfloat16
    )


def combine_rows(returned, route_fwd, gate_fwd, residual):
    picked_rows = returned[route_fwd[0]]
    combined = residual[0].astype(jnp.float32) + jnp.sum(
        gate_fwd[0][:, :, None] * picked_rows, axis=1
    )
    return combined.astype(jnp.bfloat16)


def dispatch_rows(grad_in, route_bwd, gate_bwd):
    flat_slots = route_bwd[0].reshape(-1)
    route_count = flat_slots.shape[0]
    anchor = (
        jnp.zeros((route_count,), jnp.int32)
        .at[flat_slots]
        .set(jnp.arange(route_count, dtype=jnp.int32))
    )
    outgoing = grad_in[0][anchor // TOP]
    weight_rows = gate_bwd[0].reshape(-1)[anchor].astype(jnp.bfloat16)
    return (outgoing, weight_rows)


def backward_local(received, weights_in, hidden_bwd, down_weight):
    grad_hidden = lax.dot_general(
        received, down_weight[0], (((1,), (1,)), ((), ())), preferred_element_type=jnp.float32
    )
    gate_grad = jnp.sum(hidden_bwd[0] * grad_hidden, axis=1)
    hidden_grad = (weights_in.astype(jnp.float32)[:, None] * grad_hidden).astype(jnp.bfloat16)
    return (hidden_grad[None], gate_grad[None])


def body(
    hidden_fwd,
    down_weight,
    residual,
    route_fwd,
    gate_fwd,
    hidden_bwd,
    route_bwd,
    gate_bwd,
    upstream,
):
    grad_in = from_behind(upstream, "section", -1)
    outgoing, weight_rows = dispatch_rows(grad_in, route_bwd, gate_bwd)
    projected = forward_local(hidden_fwd, down_weight)
    returned = lax.all_to_all(projected, "expert", split_axis=0, concat_axis=0, tiled=True)
    received, weights_in = (
        lax.all_to_all(outgoing, "expert", split_axis=0, concat_axis=0, tiled=True),
        lax.all_to_all(weight_rows, "expert", split_axis=0, concat_axis=0, tiled=True),
    )
    layer_out = combine_rows(returned, route_fwd, gate_fwd, residual)
    next_input = from_behind(layer_out[None], "section", 1)
    hidden_grad, gate_grad = backward_local(received, weights_in, hidden_bwd, down_weight)
    return (next_input, hidden_grad, gate_grad)


def solution(mesh):
    return jax.shard_map(
        body,
        mesh=mesh,
        in_specs=(
            P("section", "expert", None),
            P("expert", None, None),
            P("section", "expert", None),
            P("section", "expert", None),
            P("section", "expert", None),
            P("section", "expert", None),
            P("section", "expert", None),
            P("section", "expert", None),
            P("section", "expert", None),
        ),
        out_specs=(
            P("section", "expert", None),
            P("section", "expert", None),
            P("section", "expert"),
        ),
        check_vma=False,
    )
```

profile of v0, /device:TPU:0, one launch (start us, length us, event | category | flops | bytes accessed | tf_op | source)
XLA Modules:
  0.0 63.9 jit_solution(7635206286654483019)
XLA Ops:
  0.6 0.0 copy-start
  0.6 0.8 %copy.19 = bf16[1,32,8]{2,1,0:T(8,128)(2,1)S(1)} copy(f32[1,32,8]{1,2,0:T(8,128)} %param.16) | data formatting | bytes 1536 | tf_op args[7]
  1.5 0.1 reshape_squeeze.6
  1.6 0.8 %copy.20 = s32[1,32,8]{2,1,0:T(8,128)S(1)} copy(s32[1,32,8]{1,2,0:T(8,128)} %param.15) | data formatting | bytes 2048 | tf_op args[6]
  2.4 0.1 reshape_squeeze.7
  2.5 1.4 %scatter_custom_fusion = s32[256]{0:T(256)S(1)} fusion(s32[256]{0:T(256)S(1)} %bitcast.40, s32[256]{0:T(256)S(1)} %iota.3, s32[]{:T(128)} %constant.8.clone.1), kind=kCustom, calls=%fused_computation.30 | custom fusion | bytes 1028 | tf_op jit(solution)/shard_map/scatter | solution.py:35
  3.9 1.9 %gather_fusion.1 = bf16[256]{0:T(256)(128)(2,1)S(1)} fusion(bf16[256]{0:T(256)(128)(2,1)S(1)} %reshape_squeeze.6, s32[1024]{0:T(1024)S(1)} %pad_clamp_fusion.1), kind=kCustom, calls=%fused_computation.1 | custom fusion | bytes 2048 | tf_op jit(solution)/shard_map/gather | solution.py:38
  5.8 0.7 %convert_element_type.60 = bf16[8,32,1]{1,2,0:T(2,128)(2,1)} reshape(bf16[256]{0:T(256)(128)(2,1)S(1)} %gather_fusion.1) | data formatting | bytes 1024 | tf_op jit(solution)/shard_map/convert_element_type | solution.py:38
  6.5 5.2 %all-to-all-start.1 = ((bf16[8,32,1]{1,2,0:T(2,128)(2,1)}), bf16[8,32,1]{1,2,0:T(2,128)(2,1)S(1)}, u32[]{:S(2)}, u32[]{:S(2)}) async-start(bf16[8,32,1]{1,2,0:T(2,128)(2,1)} %convert_element_type.60), calls=%async_computation.1 | async-start | bytes 8192 | tf_op jit(solution)/shard_map/all_to_all | solution.py:68
  11.7 0.0 copy-done
  11.7 5.6 %fusion.4 = bf16[256,2048]{1,0:T(8,128)(2,1)} fusion(bf16[1,1536,2048]{2,1,0:T(8,128)(2,1)} %param.10, bf16[1,256,1536]{2,1,0:T(8,128)(2,1)S(1)} %copy-done), kind=kOutput, calls=%fused_computation.8 | convolution fusion | flops 1611137024 | bytes 8126464 | tf_op jit(solution)/shard_map/dot_general | solution.py:16
  17.3 0.0 copy-start.4
  17.3 0.0 all-to-all-done.1
  17.3 4.3 %all-to-all-start = ((bf16[8,32,2048]{2,1,0:T(8,128)(2,1)}), bf16[8,32,2048]{2,1,0:T(8,128)(2,1)S(1)}, u32[]{:S(2)}, u32[]{:S(2)}) async-start(bf16[8,32,2048]{2,1,0:T(8,128)(2,1)} %bitcast.3), calls=%async_computation | async-start | bytes 2097152 | tf_op jit(solution)/shard_map/all_to_all | solution.py:65
  21.6 0.0 copy-done.4
  21.6 3.7 %collective-permute-start.1 = (bf16[1,32,2048]{2,1,0:T(8,128)(2,1)S(1)}, bf16[1,32,2048]{2,1,0:T(8,128)(2,1)S(1)}, u32[]{:S(2)}, u32[]{:S(2)}) collective-permute-start(bf16[1,32,2048]{2,1,0:T(8,128)(2,1)S(1)} %copy-done.4), channel_id=1, source_target_pairs={{8,0},{16,8},{24,16},{0,24},{9,1},{17,9},{25,17},{1,25},{10,2},{18... | collective-permute-start | bytes 393224 | tf_op jit(solution)/shard_map/ppermute | solution.py:12
  25.2 3.4 %collective-permute-done.1 = bf16[1,32,2048]{2,1,0:T(8,128)(2,1)S(1)} collective-permute-done((bf16[1,32,2048]{2,1,0:T(8,128)(2,1)S(1)}, bf16[1,32,2048]{2,1,0:T(8,128)(2,1)S(1)}, u32[]{:S(2)}, u32[]{:S(2)}) %collective-permute-start.1) | collective-permute-done | bytes 131104 | tf_op jit(solution)/shard_map/ppermute | solution.py:12
  28.6 2.3 %gather_fusion.2 = bf16[256,2048]{1,0:T(8,128)(2,1)} fusion(bf16[32,2048]{1,0:T(8,128)(2,1)S(1)} %bitcast.37, s32[1024]{0:T(1024)S(1)} %pad_clamp_fusion), kind=kCustom, calls=%fused_computation.2 | custom fusion | bytes 2098176 | tf_op jit(solution)/shard_map/gather | solution.py:37
  30.9 0.0 copy-start.3
  30.9 0.0 copy-start.2
  30.9 6.0 %all-to-all-done = bf16[8,32,2048]{2,1,0:T(8,128)(2,1)S(1)} async-done(((bf16[8,32,2048]{2,1,0:T(8,128)(2,1)}), bf16[8,32,2048]{2,1,0:T(8,128)(2,1)S(1)}, u32[]{:S(2)}, u32[]{:S(2)}) %all-to-all-start) | async-done | bytes 1048608 | tf_op jit(solution)/shard_map/all_to_all | solution.py:65
  37.0 4.2 %all-to-all-start.2 = ((bf16[8,32,2048]{2,1,0:T(8,128)(2,1)}), bf16[8,32,2048]{2,1,0:T(8,128)(2,1)}, u32[]{:S(2)}, u32[]{:S(2)}) async-start(bf16[8,32,2048]{2,1,0:T(8,128)(2,1)} %bitcast.10), calls=%async_computation.2 | async-start | bytes 2097152 | tf_op jit(solution)/shard_map/all_to_all | solution.py:67
  41.2 0.0 copy-done.3
  41.2 0.1 copy.18
  41.3 0.1 reshape.94
  41.4 0.0 copy-done.2
  41.4 0.1 copy.17
  41.5 0.1 reshape.90
  41.6 0.0 copy-start.1
  41.6 1.4 %gather_fusion = bf16[256,2048]{1,0:T(8,128)(2,1)S(1)} fusion(bf16[256,2048]{1,0:T(8,128)(2,1)S(1)} %bitcast.38, s32[1024]{0:T(1024)S(1)} %pad_clamp_fusion.2), kind=kCustom, calls=%fused_computation | custom fusion | bytes 2098176 | tf_op jit(solution)/shard_map/gather | solution.py:22
  43.0 1.0 %fusion.7 = f32[32,2048]{1,0:T(8,128)S(1)} fusion(bf16[256,2048]{1,0:T(8,128)(2,1)S(1)} %gather_fusion, f32[32,8]{1,0:T(8,128)S(1)} %copy.17), kind=kLoop, calls=%fused_computation.10 | loop fusion | flops 1507328 | bytes 1311744 | tf_op jit(solution)/shard_map/reduce_sum | solution.py:23
  43.9 0.0 copy-done.1
  44.0 1.6 %collective-permute-start = (bf16[1,32,2048]{2,1,0:T(8,128)(2,1)S(1)}, bf16[1,32,2048]{2,1,0:T(8,128)(2,1)S(1)}, u32[]{:S(2)}, u32[]{:S(2)}) collective-permute-start(bf16[1,32,2048]{2,1,0:T(8,128)(2,1)S(1)} %fusion.11), channel_id=1, source_target_pairs={{24,0},{0,8},{8,16},{16,24},{25,1},{1,9},{9,17},{17,25},{26,2},{2,... | collective-permute-start | bytes 393224 | tf_op jit(solution)/shard_map/ppermute | solution.py:12
  45.6 11.0 %all-to-all-done.2 = bf16[8,32,2048]{2,1,0:T(8,128)(2,1)} async-done(((bf16[8,32,2048]{2,1,0:T(8,128)(2,1)}), bf16[8,32,2048]{2,1,0:T(8,128)(2,1)}, u32[]{:S(2)}, u32[]{:S(2)}) %all-to-all-start.2) | async-done | bytes 1048608 | tf_op jit(solution)/shard_map/all_to_all | solution.py:67
  56.6 6.7 %fusion.8 = (f32[256]{0:T(256)}, bf16[1,256,1536]{2,1,0:T(8,128)(2,1)}) fusion(bf16[1,256,1536]{2,1,0:T(8,128)(2,1)} %param.14, f32[256]{0:T(256)S(1)} %reshape.90, bf16[256,2048]{1,0:T(8,128)(2,1)} %bitcast.11, bf16[1,1536,2048]{2,1,0:T(8,128)(2,1)} %param.10), kind=kOutput, calls=%fused_computation.12 | convolution fusion | flops 1612578560 | bytes 8914944 | tf_op jit(solution)/shard_map/dot_general | solution.py:43
  63.3 0.0 collective-permute-done
  63.3 0.7 %copy.23 = bf16[1,32,2048]{2,1,0:T(8,128)(2,1)} copy(bf16[1,32,2048]{2,1,0:T(8,128)(2,1)S(1)} %collective-permute-done) | data formatting | bytes 262144
  (9 shorter events, 0.1 us)
Async XLA Ops:
  0.6 11.0 %copy-start = (bf16[1,256,1536]{2,1,0:T(8,128)(2,1)S(1)}, bf16[1,256,1536]{2,1,0:T(8,128)(2,1)}, u32[]{:S(2)}) copy-start(bf16[1,256,1536]{2,1,0:T(8,128)(2,1)} %param.9) | copy-start | bytes 2359300
  6.5 10.8 %all-to-all-start.1 = ((bf16[8,32,1]{1,2,0:T(2,128)(2,1)}), bf16[8,32,1]{1,2,0:T(2,128)(2,1)S(1)}, u32[]{:S(2)}, u32[]{:S(2)}) async-start(bf16[8,32,1]{1,2,0:T(2,128)(2,1)} %convert_element_type.60), calls=%async_computation.1 | async-start | bytes 8192 | tf_op jit(solution)/shard_map/all_to_all | solution.py:68
  17.3 4.3 %copy-start.4 = (bf16[1,32,2048]{2,1,0:T(8,128)(2,1)S(1)}, bf16[1,32,2048]{2,1,0:T(8,128)(2,1)}, u32[]{:S(2)}) copy-start(bf16[1,32,2048]{2,1,0:T(8,128)(2,1)} %param.17) | copy-start | bytes 393220
  17.3 19.7 %all-to-all-start = ((bf16[8,32,2048]{2,1,0:T(8,128)(2,1)}), bf16[8,32,2048]{2,1,0:T(8,128)(2,1)S(1)}, u32[]{:S(2)}, u32[]{:S(2)}) async-start(bf16[8,32,2048]{2,1,0:T(8,128)(2,1)} %bitcast.3), calls=%async_computation | async-start | bytes 2097152 | tf_op jit(solution)/shard_map/all_to_all | solution.py:65
  21.6 7.0 %collective-permute-start.1 = (bf16[1,32,2048]{2,1,0:T(8,128)(2,1)S(1)}, bf16[1,32,2048]{2,1,0:T(8,128)(2,1)S(1)}, u32[]{:S(2)}, u32[]{:S(2)}) collective-permute-start(bf16[1,32,2048]{2,1,0:T(8,128)(2,1)S(1)} %copy-done.4), channel_id=1, source_target_pairs={{8,0},{16,8},{24,16},{0,24},{9,1},{17,9},{25,17},{1,25},{10,2},{18... | collective-permute-start | bytes 393224 | tf_op jit(solution)/shard_map/ppermute | solution.py:12
  30.9 10.3 %copy-start.3 = (s32[1,32,8]{1,2,0:T(8,128)S(1)}, s32[1,32,8]{1,2,0:T(8,128)}, u32[]{:S(2)}) copy-start(s32[1,32,8]{1,2,0:T(8,128)} %param.12) | copy-start | bytes 3076
  30.9 10.5 %copy-start.2 = (f32[1,32,8]{1,2,0:T(8,128)S(1)}, f32[1,32,8]{1,2,0:T(8,128)}, u32[]{:S(2)}) copy-start(f32[1,32,8]{1,2,0:T(8,128)} %param.13) | copy-start | bytes 3076
  37.0 19.6 %all-to-all-start.2 = ((bf16[8,32,2048]{2,1,0:T(8,128)(2,1)}), bf16[8,32,2048]{2,1,0:T(8,128)(2,1)}, u32[]{:S(2)}, u32[]{:S(2)}) async-start(bf16[8,32,2048]{2,1,0:T(8,128)(2,1)} %bitcast.10), calls=%async_computation.2 | async-start | bytes 2097152 | tf_op jit(solution)/shard_map/all_to_all | solution.py:67
  41.6 2.3 %copy-start.1 = (bf16[1,32,2048]{2,1,0:T(8,128)(2,1)S(1)}, bf16[1,32,2048]{2,1,0:T(8,128)(2,1)}, u32[]{:S(2)}) copy-start(bf16[1,32,2048]{2,1,0:T(8,128)(2,1)} %param.11) | copy-start | bytes 393220
  44.0 19.3 %collective-permute-start = (bf16[1,32,2048]{2,1,0:T(8,128)(2,1)S(1)}, bf16[1,32,2048]{2,1,0:T(8,128)(2,1)S(1)}, u32[]{:S(2)}, u32[]{:S(2)}) collective-permute-start(bf16[1,32,2048]{2,1,0:T(8,128)(2,1)S(1)} %fusion.11), channel_id=1, source_target_pairs={{24,0},{0,8},{8,16},{16,24},{25,1},{1,9},{9,17},{17,25},{26,2},{2,... | collective-permute-start | bytes 393224 | tf_op jit(solution)/shard_map/ppermute | solution.py:12
where the time goes:
time: 64.3 us; the launch traced here: 63.9 us
  waiting for transfers between devices  20.4 us (32%)
  starting transfers between devices  19 us (30%)
  matrix products  12.2 us (19%)
  local copies, waits for them, and re-layouts  10.4 us (16%)
  other arithmetic  1.05 us (2%)
  between operations  0.77 us (1%)
    all_to_all x1, waiting for transfers between devices, body(): lax.all_to_all(outgoing, 'expert', split_axis=0, concat_axis=0, tiled=True)  11 us
    dot_general x1, matrix products, backward_local(): lax.dot_general(received, down_weight[0], (((1,), (1,)), ((), ())), prefe...  6.65 us
    all_to_all x1, waiting for transfers between devices, body(): lax.all_to_all(projected, 'expert', split_axis=0, concat_axis=0, tiled=True)  6.02 us
    dot_general x1, matrix products, forward_local(): jnp.dot(hidden_fwd[0], down_weight[0], preferred_element_type=jnp.float32)  5.59 us
    ppermute x2, starting transfers between devices, from_behind(): return lax.ppermute(block, axis, route)  5.28 us
    all_to_all x1, starting transfers between devices, body(): lax.all_to_all(weight_rows, 'expert', split_axis=0, concat_axis=0, tiled=...  5.2 us
    all_to_all x1, starting transfers between devices, body(): lax.all_to_all(projected, 'expert', split_axis=0, concat_axis=0, tiled=True)  4.33 us
    all_to_all x1, starting transfers between devices, body(): lax.all_to_all(outgoing, 'expert', split_axis=0, concat_axis=0, tiled=True)  4.24 us
  transfers between devices with their start and end apart: 5, of which 3 were waited for; matrix products, arithmetic and copies ran while one was open for 27% of the time, Pallas kernels for 0%

commit v1 on v0

v1 whole, which is shorter than its diff:
```python
import functools

import jax
import jax.numpy as jnp
from jax import lax
from jax.experimental import pallas as pl
from jax.experimental.pallas import tpu as pltpu
from jax.sharding import PartitionSpec as P

F32 = jnp.float32
BF16 = jnp.bfloat16


def from_behind(block, axis, distance):
    devices = range(lax.axis_size(axis))
    route = [((i - distance) % len(devices), i) for i in devices]
    return lax.ppermute(block, axis, route)


def forward_local(hidden_fwd, down_weight):
    return jnp.dot(hidden_fwd[0], down_weight[0], preferred_element_type=F32).astype(BF16)


def combine_rows(returned, route_fwd, gate_fwd, residual):
    picked_rows = returned[route_fwd[0]]
    combined = residual[0].astype(F32) + jnp.sum(gate_fwd[0][:, :, None] * picked_rows, axis=1)
    return combined.astype(BF16)


def dispatch_rows(grad_in, route_bwd, gate_bwd):
    top = route_bwd.shape[-1]
    flat_slots = route_bwd[0].reshape(-1)
    route_count = flat_slots.shape[0]
    anchor = (
        jnp.zeros((route_count,), jnp.int32)
        .at[flat_slots]
        .set(jnp.arange(route_count, dtype=jnp.int32))
    )
    outgoing = grad_in[0][anchor // top]
    weight_rows = gate_bwd[0].reshape(-1)[anchor].astype(BF16)
    return (outgoing, weight_rows)


def backward_local(received, weights_in, hidden_bwd, down_weight):
    grad_hidden = lax.dot_general(
        received, down_weight[0], (((1,), (1,)), ((), ())), preferred_element_type=F32
    )
    gate_grad = jnp.sum(hidden_bwd[0] * grad_hidden, axis=1)
    hidden_grad = (weights_in.astype(F32)[:, None] * grad_hidden).astype(BF16)
    return (hidden_grad[None], gate_grad[None])


def sparse_body(
    hidden_fwd, down_weight, residual, route_fwd, gate_fwd, hidden_bwd, route_bwd, gate_bwd, upstream
):
    grad_in = from_behind(upstream, "section", -1)
    outgoing, weight_rows = dispatch_rows(grad_in, route_bwd, gate_bwd)
    projected = forward_local(hidden_fwd, down_weight)
    returned = lax.all_to_all(projected, "expert", split_axis=0, concat_axis=0, tiled=True)
    received, weights_in = (
        lax.all_to_all(outgoing, "expert", split_axis=0, concat_axis=0, tiled=True),
        lax.all_to_all(weight_rows, "expert", split_axis=0, concat_axis=0, tiled=True),
    )
    layer_out = combine_rows(returned, route_fwd, gate_fwd, residual)
    next_input = from_behind(layer_out[None], "section", 1)
    hidden_grad, gate_grad = backward_local(received, weights_in, hidden_bwd, down_weight)
    return (next_input, hidden_grad, gate_grad)


def kernel(
    n, sections, nch, nbw,
    hf_ref, w_ref, res_ref, rf_ref, gf_ref, hb_ref, rb_ref, gb_ref, up_ref,
    next_ref, hg_ref, gg_ref,
    hf, w, res, hb, rt, gt, gbuf, gp, cown, csend, crecv, ssend, srecv, nout, hgs,
    ld, sm_loc, sm_send, sm_recv, z_send, z_recv, ag_send, ag_recv, fw_send, fw_recv,
    xc_send, xc_recv, rs_send, rs_recv, no_send, no_recv, out_sem,
):
    e = lax.axis_index("expert")
    s = lax.axis_index("section")
    chips = n // 2
    p = lax.div(e, 2)
    c = lax.rem(e, 2)
    mine = c * chips + p
    partner = e + 1 - 2 * c
    above = lax.rem(s + 1, sections)
    below = lax.rem(s + sections - 1, sections)
    rows, ff = hf.shape
    d = w.shape[1]
    tokens = res.shape[0]
    cap = rows // n
    half = chips * tokens
    dc = d // nch
    fb = ff // nbw

    def cols(i):
        return slice(i * dc, (i + 1) * dc)

    def remote(src, dst, ss, rs, section=None, expert=None):
        return pltpu.make_async_remote_copy(
            src_ref=src, dst_ref=dst, send_sem=ss, recv_sem=rs,
            device_id={
                "section": s if section is None else section,
                "expert": e if expert is None else expert,
            },
            device_id_type=pl.DeviceIdType.MESH,
        )

    loads = [pltpu.make_async_copy(hf_ref.at[0], hf, ld.at[nch])]
    for i in range(nch):
        loads.append(
            pltpu.make_async_copy(w_ref.at[0, :, cols(i)], w.at[:, cols(i)], ld.at[i])
        )
    loads.append(pltpu.make_async_copy(res_ref.at[0], res, ld.at[nch + 1]))
    loads.append(pltpu.make_async_copy(hb_ref.at[0], hb, ld.at[nch + 2]))
    for load in loads:
        load.start()
    tables = [(rf_ref, rt, 0), (gf_ref, gt, 0), (rb_ref, rt, 1), (gb_ref, gt, 1)]
    local = []
    for i, (src, dst, kind) in enumerate(tables):
        local.append(pltpu.make_async_copy(src, dst.at[kind, mine], sm_loc.at[i]))
        local[-1].start()

    barrier = pltpu.get_barrier_semaphore()
    for k in range(1, n):
        pl.semaphore_signal(
            barrier, inc=1, device_id={"section": s, "expert": lax.rem(e + k, n)},
            device_id_type=pl.DeviceIdType.MESH,
        )
    for other in (above, below):
        pl.semaphore_signal(
            barrier, inc=1, device_id={"section": other, "expert": e},
            device_id_type=pl.DeviceIdType.MESH,
        )
    pl.semaphore_wait(barrier, n + 1)

    zs = []
    for i in range(nch):
        zs.append(
            remote(up_ref.at[0, :, cols(i)], gbuf.at[c, p, :, cols(i)],
                   z_send.at[i], z_recv.at[i], section=below)
        )
        zs[-1].start()
    small = []
    for i, (src, dst, kind) in enumerate(tables):
        for k in range(1, n):
            small.append(
                remote(src, dst.at[kind, mine], sm_send.at[i, k - 1], sm_recv.at[i, k - 1],
                       expert=lax.rem(e + k, n))
            )
            small[-1].start()

    drains = []

    def send(copy):
        copy.start()
        drains.append(copy)
        return copy

    def peer(k):
        return 2 * lax.rem(p + k, chips) + c

    def gather_out(i):
        zs[i].wait_recv()
        block = gbuf.at[c, p, :, cols(i)]
        for k in range(1, chips):
            send(remote(block, block, ag_send.at[k - 1, i], ag_recv.at[k - 1, i], expert=peer(k)))
        send(remote(block, block, fw_send.at[0, i], fw_recv.at[0, i], expert=partner))

    def gather_forward(k, i):
        block = gbuf.at[c, lax.rem(p + chips - k, chips), :, cols(i)]
        remote(block, block, ag_send.at[k - 1, i], ag_recv.at[k - 1, i], expert=partner).wait_recv()
        send(remote(block, block, fw_send.at[k, i], fw_recv.at[k, i], expert=partner))

    def gather_done(k, i):
        block = gbuf.at[1 - c, lax.rem(p + chips - k, chips), :, cols(i)]
        remote(block, block, fw_send.at[k, i], fw_recv.at[k, i], expert=partner).wait_recv()

    def project(i):
        loads[1 + i].wait()
        return jnp.dot(hf[...], w[:, cols(i)], preferred_element_type=F32).astype(BF16)

    loads[0].wait()
    out = project(0)

    for copy in local:
        copy.wait()
    for copy in small:
        copy.wait_recv()

    def table(ref, kind):
        return jnp.concatenate([ref[kind, q] for q in range(n)], axis=1)

    lo = e * cap
    lane = lax.broadcasted_iota(jnp.int32, (1, n * tokens), 1)
    lane_q = lane // tokens
    lane_base = (2 * (lane_q % chips) + lane_q // chips) * cap

    route = table(rt, 0)
    hit = (route >= lo) & (route < lo + cap)
    pos = jnp.where(hit, route - lo, 0).astype(F32).T
    gate_col = jnp.sum(jnp.where(hit, table(gt, 0), 0.0).T, axis=1, keepdims=True)
    row = lax.broadcasted_iota(jnp.int32, (n * tokens, 1), 0)
    row_q = row // tokens
    want = (2 * (row_q % chips) + row_q // chips) * cap + jnp.sum(
        pos, axis=1, keepdims=True
    ).astype(jnp.int32)
    pick = jnp.where(
        lax.broadcasted_iota(jnp.int32, (n * tokens, rows), 1) == want, 1.0, 0.0
    ).astype(BF16)

    def weigh(i, out):
        got = gate_col * jnp.dot(pick, out, preferred_element_type=F32)
        low, high = got[:half], got[half:]
        cown[:, cols(i)] = jnp.where(c == 0, low, high)
        csend[:, cols(i)] = jnp.where(c == 0, high, low).astype(BF16)
        return send(
            remote(csend.at[:, cols(i)], crecv.at[:, cols(i)], xc_send.at[i], xc_recv.at[i],
                   expert=partner)
        )

    pairs = []
    for i in range(nch):
        if i:
            out = project(i)
        pairs.append(weigh(i, out))
        gather_out(i)

    rs = {}
    for i in range(nch):
        pairs[i].wait_recv()
        total = cown[:, cols(i)] + crecv[:, cols(i)].astype(F32)
        cown[:, cols(i)] = total
        for q in range(chips):
            ssend[q, :, cols(i)] = total[q * tokens:(q + 1) * tokens].astype(BF16)
        for k in range(1, chips):
            rs[k, i] = send(
                remote(ssend.at[lax.rem(p + k, chips), :, cols(i)],
                       srecv.at[k - 1, :, cols(i)],
                       rs_send.at[k - 1, i], rs_recv.at[k - 1, i], expert=peer(k))
            )

    for i in range(nch):
        for k in range(1, chips):
            gather_forward(k, i)

    route = table(rt, 1)
    hit = (route >= lo) & (route < lo + cap)
    slot = jnp.sum(jnp.where(hit, route - lo, 0), axis=0, keepdims=True)
    gate_row = jnp.sum(jnp.where(hit, table(gt, 1), 0.0), axis=0, keepdims=True)
    match = lax.broadcasted_iota(jnp.int32, (rows, n * tokens), 0) == lane_base + slot
    weight_col = jnp.sum(jnp.where(match, gate_row, 0.0), axis=1, keepdims=True)
    weight_col = weight_col.astype(BF16).astype(F32)
    place = jnp.where(match, 1.0, 0.0).astype(BF16)

    for i in range(nch):
        for k in range(chips):
            gather_done(k, i)
        tok = gbuf[:, :, :, cols(i)].reshape(n * tokens, dc)
        gp[:, cols(i)] = jnp.dot(place, tok, preferred_element_type=F32).astype(BF16)

    loads[nch + 1].wait()
    loads[nch + 2].wait()
    nos = []

    def finish(i):
        total = cown[pl.ds(pl.multiple_of(p * tokens, tokens), tokens), cols(i)]
        total = res[:, cols(i)].astype(F32) + total
        for k in range(1, chips):
            rs[k, i].wait_recv()
            total = total + srecv[k - 1, :, cols(i)].astype(F32)
        nout[:, cols(i)] = total.astype(BF16)
        nos.append(
            send(remote(nout.at[:, cols(i)], next_ref.at[0, :, cols(i)],
                        no_send.at[i], no_recv.at[i], section=above))
        )

    outs = []
    gate_sum = jnp.zeros((rows, 1), F32)
    done = 0
    for j in range(nbw):
        span = slice(j * fb, (j + 1) * fb)
        grad = lax.dot_general(
            gp[...], w[span, :], (((1,), (1,)), ((), ())), preferred_element_type=F32
        )
        gate_sum = gate_sum + jnp.sum(hb[:, span].astype(F32) * grad, axis=1, keepdims=True)
        hgs[:, span] = (weight_col * grad).astype(BF16)
        outs.append(
            pltpu.make_async_copy(hgs.at[:, span], hg_ref.at[0, :, span], out_sem.at[j])
        )
        outs[-1].start()
        if done < nch:
            finish(done)
            done += 1
    while done < nch:
        finish(done)
        done += 1
    gg_ref[...] = jnp.broadcast_to(gate_sum, (rows, 128)).T[0:1]

    for copy in nos:
        copy.wait_recv()
    for copy in outs:
        copy.wait()
    for copy in zs + small + drains:
        copy.wait_send()


def dense_body(
    hidden_fwd, down_weight, residual, route_fwd, gate_fwd, hidden_bwd, route_bwd, gate_bwd, upstream
):
    n = lax.axis_size("expert")
    sections = lax.axis_size("section")
    _, rows, ff = hidden_fwd.shape
    d = down_weight.shape[2]
    tokens, top = route_fwd.shape[1:]
    chips = n // 2
    nch, nbw = 4, 3
    half = chips * tokens
    dma = pltpu.SemaphoreType.DMA
    hbm = pl.BlockSpec(memory_space=pl.ANY)
    return pl.pallas_call(
        functools.partial(kernel, n, sections, nch, nbw),
        out_shape=(
            jax.ShapeDtypeStruct((1, tokens, d), BF16),
            jax.ShapeDtypeStruct((1, rows, ff), BF16),
            jax.ShapeDtypeStruct((1, rows), F32),
        ),
        in_specs=[hbm] * 9,
        out_specs=(hbm, hbm, pl.BlockSpec(memory_space=pltpu.VMEM)),
        scratch_shapes=[
            pltpu.VMEM((rows, ff), BF16),
            pltpu.VMEM((ff, d), BF16),
            pltpu.VMEM((tokens, d), BF16),
            pltpu.VMEM((rows, ff), BF16),
            pltpu.VMEM((2, n, top, tokens), jnp.int32),
            pltpu.VMEM((2, n, top, tokens), F32),
            pltpu.VMEM((2, chips, tokens, d), BF16),
            pltpu.VMEM((rows, d), BF16),
            pltpu.VMEM((half, d), F32),
            pltpu.VMEM((half, d), BF16),
            pltpu.VMEM((half, d), BF16),
            pltpu.VMEM((chips, tokens, d), BF16),
            pltpu.VMEM((chips - 1, tokens, d), BF16),
            pltpu.VMEM((tokens, d), BF16),
            pltpu.VMEM((rows, ff), BF16),
            dma((nch + 3,)),
            dma((4,)),
            dma((4, n - 1)),
            dma((4, n - 1)),
            dma((nch,)),
            dma((nch,)),
            dma((chips - 1, nch)),
            dma((chips - 1, nch)),
            dma((chips, nch)),
            dma((chips, nch)),
            dma((nch,)),
            dma((nch,)),
            dma((chips - 1, nch)),
            dma((chips - 1, nch)),
            dma((nch,)),
            dma((nch,)),
            dma((nbw,)),
        ],
        compiler_params=pltpu.CompilerParams(
            collective_id=0, has_side_effects=True, vmem_limit_bytes=60 << 20
        ),
    )(
        hidden_fwd, down_weight, residual, route_fwd[0].T, gate_fwd[0].T, hidden_bwd,
        route_bwd[0].T, gate_bwd[0].T, upstream,
    )


def body(*args):
    n = lax.axis_size("expert")
    dense = args[3].shape[2] == n and n % 2 == 0 and lax.axis_size("section") > 2
    return (dense_body if dense else sparse_body)(*args)


def solution(mesh):
    wide = P("section", "expert", None)
    return jax.shard_map(
        body,
        mesh=mesh,
        in_specs=(wide, P("expert", None, None), wide, wide, wide, wide, wide, wide, wide),
        out_specs=(wide, wide, P("section", "expert")),
        check_vma=False,
    )
```

time: 64.3 us -> 35.6 us (0.55)
  Pallas kernels: 0 us -> 29.9 us
  waiting for transfers between devices: 20.4 us -> 0 us
  starting transfers between devices: 19 us -> 0 us
  matrix products: 12.2 us -> 0 us
  local copies, waits for them, and re-layouts: 10.4 us -> 4.87 us
  other arithmetic: 1.05 us -> 0 us
    pallas_call x0 -> x1, Pallas kernels: none -> 29.9 us  [dense_body(): pl.pallas_call(functools.partial(kernel, n, sections, nch, nbw), out_shap...]
    all_to_all x3 -> x0, waiting for transfers between devices: 17 us -> none  [the longest x1 11 us: body(): lax.all_to_all(outgoing, 'expert', split_axis=0, concat_axis=0, tiled=True)]
    all_to_all x3 -> x0, starting transfers between devices: 13.8 us -> none  [the longest x1 5.2 us: body(): lax.all_to_all(weight_rows, 'expert', split_axis=0, concat_axis=0, tiled=...]
    dot_general x2 -> x0, matrix products: 12.2 us -> none  [the longest x1 6.65 us: backward_local(): lax.dot_general(received, down_weight[0], (((1,), (1,)), ((), ())), prefe...]
    gather x3 -> x0, local copies, waits for them, and re-layouts: 5.55 us -> none  [the longest x1 2.32 us: dispatch_rows(): outgoing = grad_in[0][anchor // TOP]]
    ppermute x2 -> x0, starting transfers between devices: 5.28 us -> none  [from_behind(): return lax.ppermute(block, axis, route)]
    ppermute x2 -> x0, waiting for transfers between devices: 3.37 us -> none  [from_behind(): return lax.ppermute(block, axis, route)]
    unnamed x13 -> x3, local copies, waits for them, and re-layouts: 2.29 us -> 4.87 us
  transfers between devices with their start and end apart: 5 -> 0, of which waited for: 3 -> 0; matrix products, arithmetic and copies ran while one was open for 27% -> 0% of each run, Pallas kernels for 0% -> 0%
where the time goes in v1:
time: 35.6 us; the launch traced here: 35.4 us
  Pallas kernels  29.9 us (84%)
  local copies, waits for them, and re-layouts  4.87 us (14%)
  between operations  0.64 us (2%)
    pallas_call x1, Pallas kernels, dense_body(): pl.pallas_call(functools.partial(kernel, n, sections, nch, nbw), out_shap...  29.9 us
    unnamed x3, local copies, waits for them, and re-layouts  4.87 us

profile of v1, /device:TPU:0, one launch (start us, length us, event | category | flops | bytes accessed | tf_op | source)
XLA Modules:
  0.0 35.4 jit_solution(4335202447595660602)
XLA Ops:
  0.6 29.9 %shard_map.112 = (bf16[1,32,2048]{2,1,0:T(8,128)(2,1)}, bf16[1,256,1536]{2,1,0:T(8,128)(2,1)}, f32[1,256]{1,0:T(1,128)}) custom-call(bf16[1,256,1536]{2,1,0:T(8,128)(2,1)} %hf_ref.1, bf16[1,1536,2048]{2,1,0:T(8,128)(2,1)} %w_ref.1, bf16[1,32,2048]{2,1,0:T(8,128)(2,1)} %res_ref.1, s32[8,32]{1,0:T(8,128)} %bitcast.12, f32[8,32]{1,0:T(8,128)} %bitcast.13, ...), custom_call_target="tpu_custom_call" | custom-call | tf_op jit(solution)/shard_map/pallas_call | solution.py:320
  30.5 1.6 %copy.15 = bf16[1,32,2048]{2,1,0:T(8,128)(2,1)} copy(bf16[1,32,2048]{2,1,0:T(8,128)(2,1)} %get-tuple-element.6) | data formatting | bytes 262144
  32.1 2.1 %copy.16 = bf16[1,256,1536]{2,1,0:T(8,128)(2,1)} copy(bf16[1,256,1536]{2,1,0:T(8,128)(2,1)} %get-tuple-element.7) | data formatting | bytes 1572864
  34.1 1.2 %copy.17 = f32[1,256]{1,0:T(1,128)} copy(f32[1,256]{1,0:T(1,128)} %get-tuple-element.8) | data formatting | bytes 2048

commit v2 on v1

v2 whole, which is shorter than its diff:
```python
import functools

import jax
import jax.numpy as jnp
from jax import lax
from jax.experimental import pallas as pl
from jax.experimental.pallas import tpu as pltpu
from jax.sharding import PartitionSpec as P

F32 = jnp.float32
BF16 = jnp.bfloat16


def from_behind(block, axis, distance):
    devices = range(lax.axis_size(axis))
    route = [((i - distance) % len(devices), i) for i in devices]
    return lax.ppermute(block, axis, route)


def forward_local(hidden_fwd, down_weight):
    return jnp.dot(hidden_fwd[0], down_weight[0], preferred_element_type=F32).astype(BF16)


def combine_rows(returned, route_fwd, gate_fwd, residual):
    picked_rows = returned[route_fwd[0]]
    combined = residual[0].astype(F32) + jnp.sum(gate_fwd[0][:, :, None] * picked_rows, axis=1)
    return combined.astype(BF16)


def dispatch_rows(grad_in, route_bwd, gate_bwd):
    top = route_bwd.shape[-1]
    flat_slots = route_bwd[0].reshape(-1)
    route_count = flat_slots.shape[0]
    anchor = (
        jnp.zeros((route_count,), jnp.int32)
        .at[flat_slots]
        .set(jnp.arange(route_count, dtype=jnp.int32))
    )
    outgoing = grad_in[0][anchor // top]
    weight_rows = gate_bwd[0].reshape(-1)[anchor].astype(BF16)
    return (outgoing, weight_rows)


def backward_local(received, weights_in, hidden_bwd, down_weight):
    grad_hidden = lax.dot_general(
        received, down_weight[0], (((1,), (1,)), ((), ())), preferred_element_type=F32
    )
    gate_grad = jnp.sum(hidden_bwd[0] * grad_hidden, axis=1)
    hidden_grad = (weights_in.astype(F32)[:, None] * grad_hidden).astype(BF16)
    return (hidden_grad[None], gate_grad[None])


def sparse_body(
    hidden_fwd, down_weight, residual, route_fwd, gate_fwd, hidden_bwd, route_bwd, gate_bwd, upstream
):
    grad_in = from_behind(upstream, "section", -1)
    outgoing, weight_rows = dispatch_rows(grad_in, route_bwd, gate_bwd)
    projected = forward_local(hidden_fwd, down_weight)
    returned = lax.all_to_all(projected, "expert", split_axis=0, concat_axis=0, tiled=True)
    received, weights_in = (
        lax.all_to_all(outgoing, "expert", split_axis=0, concat_axis=0, tiled=True),
        lax.all_to_all(weight_rows, "expert", split_axis=0, concat_axis=0, tiled=True),
    )
    layer_out = combine_rows(returned, route_fwd, gate_fwd, residual)
    next_input = from_behind(layer_out[None], "section", 1)
    hidden_grad, gate_grad = backward_local(received, weights_in, hidden_bwd, down_weight)
    return (next_input, hidden_grad, gate_grad)


def kernel(
    n, sections, nch, nag, nbw,
    hf_ref, w_ref, res_ref, rf_ref, gf_ref, hb_ref, rb_ref, gb_ref, up_ref,
    next_ref, hg_ref, gg_ref,
    hf, w, res, hb, ti, tf, pack, tab, gbuf, gp, cown, csend, crecv, ssend, smid, r1a, r1b, r2,
    nout, hgs,
    ld, sm_loc, sm_send, sm_recv, z_send, z_recv, ag_send, ag_recv, fw_send, fw_recv,
    xc_send, xc_recv, rs_send, rs_recv, no_send, no_recv, out_sem,
):
    e = lax.axis_index("expert")
    s = lax.axis_index("section")
    chips = n // 2
    p = lax.div(e, 2)
    c = lax.rem(e, 2)
    mine = c * chips + p
    partner = e + 1 - 2 * c
    above = lax.rem(s + 1, sections)
    below = lax.rem(s + sections - 1, sections)
    beside_x = p + 1 - 2 * lax.rem(p, 2)
    beside_y = lax.rem(p + 2, chips)
    across = chips - 1 - p
    rows, ff = hf.shape
    d = w.shape[1]
    tokens = res.shape[0]
    cap = rows // n
    half = chips * tokens
    dc = d // nch
    ta = tokens // nag
    fb = ff // nbw

    def cols(i):
        return slice(i * dc, (i + 1) * dc)

    def part(i):
        return slice(i * ta, (i + 1) * ta)

    def of_chip(q):
        return pl.ds(pl.multiple_of(q * tokens, tokens), tokens)

    def remote(src, dst, ss, rs, section=None, expert=None):
        return pltpu.make_async_remote_copy(
            src_ref=src, dst_ref=dst, send_sem=ss, recv_sem=rs,
            device_id={
                "section": s if section is None else section,
                "expert": e if expert is None else expert,
            },
            device_id_type=pl.DeviceIdType.MESH,
        )

    barrier = pltpu.get_barrier_semaphore()
    for k in range(1, n):
        pl.semaphore_signal(
            barrier, inc=1, device_id={"section": s, "expert": lax.rem(e + k, n)},
            device_id_type=pl.DeviceIdType.MESH,
        )
    for other in (above, below):
        pl.semaphore_signal(
            barrier, inc=1, device_id={"section": other, "expert": e},
            device_id_type=pl.DeviceIdType.MESH,
        )
    local = []
    for i, (src, dst) in enumerate(
        [(rf_ref, ti.at[0]), (gf_ref, tf.at[0]), (rb_ref, ti.at[1]), (gb_ref, tf.at[1])]
    ):
        local.append(pltpu.make_async_copy(src, dst, sm_loc.at[i]))
        local[-1].start()
    loads = [pltpu.make_async_copy(hf_ref.at[0], hf, ld.at[nch])]
    for i in range(nch):
        loads.append(
            pltpu.make_async_copy(w_ref.at[0, :, cols(i)], w.at[:, cols(i)], ld.at[i])
        )
    loads.append(pltpu.make_async_copy(res_ref.at[0], res, ld.at[nch + 1]))
    loads.append(pltpu.make_async_copy(hb_ref.at[0], hb, ld.at[nch + 2]))
    for load in loads:
        load.start()
    for copy in local:
        copy.wait()
    packed = jnp.concatenate([ti[0].astype(F32), tf[0], ti[1].astype(F32), tf[1]], axis=1)
    pack[...] = packed
    tab[mine] = packed
    pl.semaphore_wait(barrier, n + 1)

    drains = []

    def send(copy):
        copy.start()
        drains.append(copy)
        return copy

    zs = []
    for i in range(nag):
        zs.append(
            send(remote(up_ref.at[0, part(i)], gbuf.at[c, p, part(i)],
                        z_send.at[i], z_recv.at[i], section=below))
        )
    small = []
    for k in range(1, n):
        small.append(
            send(remote(pack, tab.at[mine], sm_send.at[k - 1], sm_recv.at[k - 1],
                        expert=lax.rem(e + k, n)))
        )

    def expert_at(q):
        return 2 * q + c

    def block(q, i, core=None):
        return gbuf.at[c if core is None else core, q, part(i)]

    def gather(q, j, i, to):
        ref = block(q, i)
        return remote(ref, ref, ag_send.at[j, i], ag_recv.at[j, i], expert=expert_at(to))

    def hand_over(q, j, i, core=None):
        ref = block(q, i, core)
        return remote(ref, ref, fw_send.at[j, i], fw_recv.at[j, i], expert=partner)

    def gather_out(i):
        zs[i].wait_recv()
        send(gather(p, 0, i, beside_x))
        send(gather(p, 1, i, beside_y))
        send(hand_over(p, 0, i))

    def gather_near(i):
        gather(beside_x, 0, i, beside_x).wait_recv()
        if i % 2 == 0:
            send(gather(beside_x, 2, i, beside_y))
        send(hand_over(beside_x, 1, i))
        gather(beside_y, 1, i, beside_y).wait_recv()
        if i % 2 == 1:
            send(gather(beside_y, 2, i, beside_x))
        send(hand_over(beside_y, 2, i))

    def gather_far(i):
        gather(across, 2, i, beside_x).wait_recv()
        send(hand_over(across, 3, i))

    def gather_done(i):
        for j, q in enumerate((p, beside_x, beside_y, across)):
            hand_over(q, j, i, 1 - c).wait_recv()

    def project(i):
        loads[1 + i].wait()
        return jnp.dot(hf[...], w[:, cols(i)], preferred_element_type=F32).astype(BF16)

    loads[0].wait()
    out = project(0)
    for copy in small:
        copy.wait_recv()

    def table(kind):
        span = slice(kind * tokens, (kind + 1) * tokens)
        return jnp.concatenate([tab[q, :, span] for q in range(n)], axis=1)

    lo = e * cap
    lane = lax.broadcasted_iota(jnp.int32, (1, n * tokens), 1)
    lane_q = lane // tokens
    lane_base = (2 * (lane_q % chips) + lane_q // chips) * cap

    route = table(0).astype(jnp.int32)
    hit = (route >= lo) & (route < lo + cap)
    pos = jnp.where(hit, route - lo, 0).astype(F32).T
    gate_col = jnp.sum(jnp.where(hit, table(1), 0.0).T, axis=1, keepdims=True)
    row = lax.broadcasted_iota(jnp.int32, (n * tokens, 1), 0)
    row_q = row // tokens
    want = (2 * (row_q % chips) + row_q // chips) * cap + jnp.sum(
        pos, axis=1, keepdims=True
    ).astype(jnp.int32)
    pick = jnp.where(
        lax.broadcasted_iota(jnp.int32, (n * tokens, rows), 1) == want, 1.0, 0.0
    ).astype(BF16)

    def weigh(i, out):
        got = gate_col * jnp.dot(pick, out, preferred_element_type=F32)
        low, high = got[:half], got[half:]
        cown[:, cols(i)] = jnp.where(c == 0, low, high)
        csend[:, cols(i)] = jnp.where(c == 0, high, low).astype(BF16)
        return send(
            remote(csend.at[:, cols(i)], crecv.at[:, cols(i)], xc_send.at[i], xc_recv.at[i],
                   expert=partner)
        )

    def first_second(i):
        return (beside_x, beside_y) if i % 2 == 0 else (beside_y, beside_x)

    far, near, last, nos = {}, {}, {}, []

    def scatter_out(i):
        first, _ = first_second(i)
        pairs[i].wait_recv()
        total = cown[:, cols(i)] + crecv[:, cols(i)].astype(F32)
        cown[:, cols(i)] = total
        ssend[:, cols(i)] = total.astype(BF16)
        far[i] = send(remote(ssend.at[of_chip(across), cols(i)], r1a.at[:, cols(i)],
                             rs_send.at[0, i], rs_recv.at[0, i], expert=expert_at(first)))
        near[i] = send(remote(ssend.at[of_chip(first), cols(i)], r1b.at[:, cols(i)],
                              rs_send.at[1, i], rs_recv.at[1, i], expert=expert_at(first)))

    def scatter_mid(i):
        _, second = first_second(i)
        far[i].wait_recv()
        both = cown[of_chip(second), cols(i)] + r1a[:, cols(i)].astype(F32)
        smid[:, cols(i)] = both.astype(BF16)
        last[i] = send(remote(smid.at[:, cols(i)], r2.at[:, cols(i)],
                              rs_send.at[2, i], rs_recv.at[2, i], expert=expert_at(second)))

    def finish(i):
        near[i].wait_recv()
        total = res[:, cols(i)].astype(F32) + cown[of_chip(p), cols(i)]
        total = total + r1b[:, cols(i)].astype(F32)
        last[i].wait_recv()
        total = total + r2[:, cols(i)].astype(F32)
        nout[:, cols(i)] = total.astype(BF16)
        nos.append(
            send(remote(nout.at[:, cols(i)], next_ref.at[0, :, cols(i)],
                        no_send.at[i], no_recv.at[i], section=above))
        )

    pairs = []
    for i in range(nch):
        if i:
            out = project(i)
        pairs.append(weigh(i, out))
        if i >= 1:
            scatter_out(i - 1)
        if i < nag:
            gather_out(i)
    scatter_out(nch - 1)
    for i in range(nag):
        gather_near(i)
    for i in range(nch):
        scatter_mid(i)
    for i in range(nag):
        gather_far(i)

    route = table(2).astype(jnp.int32)
    hit = (route >= lo) & (route < lo + cap)
    slot = jnp.sum(jnp.where(hit, route - lo, 0), axis=0, keepdims=True)
    gate_row = jnp.sum(jnp.where(hit, table(3), 0.0), axis=0, keepdims=True)
    match = lax.broadcasted_iota(jnp.int32, (rows, n * tokens), 0) == lane_base + slot
    weight_col = jnp.sum(jnp.where(match, gate_row, 0.0), axis=1, keepdims=True)
    weight_col = weight_col.astype(BF16).astype(F32)
    place = jnp.where(match, 1.0, 0.0).astype(BF16)

    loads[nch + 1].wait()
    loads[nch + 2].wait()
    for i in range(nch):
        finish(i)
    for i in range(nag):
        gather_done(i)
    for i in range(nch):
        tok = gbuf[:, :, :, cols(i)].reshape(n * tokens, dc)
        gp[:, cols(i)] = jnp.dot(place, tok, preferred_element_type=F32).astype(BF16)

    outs = []
    gate_sum = jnp.zeros((rows, 1), F32)
    for j in range(nbw):
        span = slice(j * fb, (j + 1) * fb)
        grad = lax.dot_general(
            gp[...], w[span, :], (((1,), (1,)), ((), ())), preferred_element_type=F32
        )
        gate_sum = gate_sum + jnp.sum(hb[:, span].astype(F32) * grad, axis=1, keepdims=True)
        hgs[:, span] = (weight_col * grad).astype(BF16)
        outs.append(
            pltpu.make_async_copy(hgs.at[:, span], hg_ref.at[0, :, span], out_sem.at[j])
        )
        outs[-1].start()
    gg_ref[...] = jnp.broadcast_to(gate_sum, (rows, 128)).T[0:1]

    for copy in nos:
        copy.wait_recv()
    for copy in outs:
        copy.wait()
    for copy in drains:
        copy.wait_send()


def publish_kernel(*refs):
    count = 3
    sources, targets, held = refs[:count], refs[count:2 * count], refs[2 * count:3 * count]
    into, out = refs[3 * count:]
    ins = [pltpu.make_async_copy(sources[i], held[i], into.at[i]) for i in range(count)]
    outs = [pltpu.make_async_copy(held[i], targets[i], out.at[i]) for i in range(count)]
    for copy in ins:
        copy.start()
    for i in (0, 2, 1):
        ins[i].wait()
        outs[i].start()
    for copy in outs:
        copy.wait()


def publish(*arrays):
    hbm = pl.BlockSpec(memory_space=pl.ANY)
    return pl.pallas_call(
        publish_kernel,
        out_shape=tuple(jax.ShapeDtypeStruct(a.shape, a.dtype) for a in arrays),
        in_specs=[hbm] * len(arrays),
        out_specs=(hbm,) * len(arrays),
        scratch_shapes=[pltpu.VMEM(a.shape, a.dtype) for a in arrays]
        + [pltpu.SemaphoreType.DMA((len(arrays),))] * 2,
    )(*arrays)


def dense_body(
    hidden_fwd, down_weight, residual, route_fwd, gate_fwd, hidden_bwd, route_bwd, gate_bwd, upstream
):
    n = lax.axis_size("expert")
    sections = lax.axis_size("section")
    _, rows, ff = hidden_fwd.shape
    d = down_weight.shape[2]
    tokens, top = route_fwd.shape[1:]
    chips = n // 2
    nch, nag, nbw = 4, 2, 3
    half = chips * tokens
    dma = pltpu.SemaphoreType.DMA
    hbm = pl.BlockSpec(memory_space=pl.ANY)
    results = pl.pallas_call(
        functools.partial(kernel, n, sections, nch, nag, nbw),
        out_shape=(
            jax.ShapeDtypeStruct((1, tokens, d), BF16),
            jax.ShapeDtypeStruct((1, rows, ff), BF16),
            jax.ShapeDtypeStruct((1, rows), F32),
        ),
        in_specs=[hbm] * 9,
        out_specs=(hbm, hbm, pl.BlockSpec(memory_space=pltpu.VMEM)),
        scratch_shapes=[
            pltpu.VMEM((rows, ff), BF16),
            pltpu.VMEM((ff, d), BF16),
            pltpu.VMEM((tokens, d), BF16),
            pltpu.VMEM((rows, ff), BF16),
            pltpu.VMEM((2, top, tokens), jnp.int32),
            pltpu.VMEM((2, top, tokens), F32),
            pltpu.VMEM((top, 4 * tokens), F32),
            pltpu.VMEM((n, top, 4 * tokens), F32),
            pltpu.VMEM((2, chips, tokens, d), BF16),
            pltpu.VMEM((rows, d), BF16),
            pltpu.VMEM((half, d), F32),
            pltpu.VMEM((half, d), BF16),
            pltpu.VMEM((half, d), BF16),
            pltpu.VMEM((half, d), BF16),
            pltpu.VMEM((tokens, d), BF16),
            pltpu.VMEM((tokens, d), BF16),
            pltpu.VMEM((tokens, d), BF16),
            pltpu.VMEM((tokens, d), BF16),
            pltpu.VMEM((tokens, d), BF16),
            pltpu.VMEM((rows, ff), BF16),
            dma((nch + 3,)),
            dma((4,)),
            dma((n - 1,)),
            dma((n - 1,)),
            dma((nag,)),
            dma((nag,)),
            dma((3, nag)),
            dma((3, nag)),
            dma((4, nag)),
            dma((4, nag)),
            dma((nch,)),
            dma((nch,)),
            dma((3, nch)),
            dma((3, nch)),
            dma((nch,)),
            dma((nch,)),
            dma((nbw,)),
        ],
        compiler_params=pltpu.CompilerParams(
            collective_id=0, has_side_effects=True, vmem_limit_bytes=60 << 20
        ),
    )(
        hidden_fwd, down_weight, residual, route_fwd[0].T, gate_fwd[0].T, hidden_bwd,
        route_bwd[0].T, gate_bwd[0].T, upstream,
    )
    return publish(*results)


def body(*args):
    n = lax.axis_size("expert")
    dense = args[3].shape[2] == n and n // 2 == 4 and lax.axis_size("section") > 2
    return (dense_body if dense else sparse_body)(*args)


def solution(mesh):
    wide = P("section", "expert", None)
    return jax.shard_map(
        body,
        mesh=mesh,
        in_specs=(wide, P("expert", None, None), wide, wide, wide, wide, wide, wide, wide),
        out_specs=(wide, wide, P("section", "expert")),
        check_vma=False,
    )
```

time: 35.6 us -> 30.7 us (0.86)
  local copies, waits for them, and re-layouts: 4.87 us -> 0 us
    unnamed x3 -> x0, local copies, waits for them, and re-layouts: 4.87 us -> none
    pallas_call x1 -> x2, Pallas kernels: 29.9 us -> 29.9 us  [the longest x1 27.8 us: dense_body(): pl.pallas_call(functools.partial(kernel, n, sections, nch, nag, nbw), out...]
where the time goes in v2:
time: 30.7 us; the launch traced here: 30.6 us
  Pallas kernels  29.9 us (97%)
  between operations  0.64 us (2%)
    pallas_call x1, Pallas kernels, dense_body(): pl.pallas_call(functools.partial(kernel, n, sections, nch, nag, nbw), out...  27.8 us
    pallas_call x1, Pallas kernels, publish(): pl.pallas_call(publish_kernel, out_shape=tuple((jax.ShapeDtypeStruct(a.sh...  2.14 us

profile of v2, /device:TPU:0, one launch (start us, length us, event | category | flops | bytes accessed | tf_op | source)
XLA Modules:
  0.0 30.6 jit_solution(16835795636624855775)
XLA Ops:
  0.6 27.8 %shard_map.112 = (bf16[1,32,2048]{2,1,0:T(8,128)(2,1)}, bf16[1,256,1536]{2,1,0:T(8,128)(2,1)}, f32[1,256]{1,0:T(1,128)}) custom-call(bf16[1,256,1536]{2,1,0:T(8,128)(2,1)} %hf_ref.1, bf16[1,1536,2048]{2,1,0:T(8,128)(2,1)} %w_ref.1, bf16[1,32,2048]{2,1,0:T(8,128)(2,1)} %res_ref.1, s32[8,32]{1,0:T(8,128)} %bitcast.12, f32[8,32]{1,0:T(8,128)} %bitcast.13, ...), custom_call_target="tpu_custom_call" | custom-call | tf_op jit(solution)/shard_map/pallas_call | solution.py:386
  28.4 2.1 %shard_map.113 = (bf16[1,32,2048]{2,1,0:T(8,128)(2,1)}, bf16[1,256,1536]{2,1,0:T(8,128)(2,1)}, f32[1,256]{1,0:T(1,128)}) custom-call(bf16[1,32,2048]{2,1,0:T(8,128)(2,1)} %get-tuple-element.6.refs_0_, bf16[1,256,1536]{2,1,0:T(8,128)(2,1)} %get-tuple-element.7.refs_1_, f32[1,256]{1,0:T(1,128)} %get-tuple-element.8.refs_2_), custom_call_target="tpu_custom_call" | custom-call | tf_op jit(solution)/shard_map/pallas_call | solution.py:363

commit v3 on v2

--- a/solution.py
+++ b/solution.py
@@ -71,7 +71,7 @@
     n, sections, nch, nag, nbw,
     hf_ref, w_ref, res_ref, rf_ref, gf_ref, hb_ref, rb_ref, gb_ref, up_ref,
     next_ref, hg_ref, gg_ref,
-    hf, w, res, hb, ti, tf, pack, tab, gbuf, gp, cown, csend, crecv, ssend, smid, r1a, r1b, r2,
+    up, hf, w, res, hb, ti, tf, pack, tab, gbuf, gp, cown, csend, crecv, ssend, smid, r1a, r1b, r2,
     nout, hgs,
     ld, sm_loc, sm_send, sm_recv, z_send, z_recv, ag_send, ag_recv, fw_send, fw_recv,
     xc_send, xc_recv, rs_send, rs_recv, no_send, no_recv, out_sem,
@@ -127,7 +127,8 @@
             barrier, inc=1, device_id={"section": other, "expert": e},
             device_id_type=pl.DeviceIdType.MESH,
         )
-    local = []
+    local = [pltpu.make_async_copy(up_ref.at[0], up, sm_loc.at[4])]
+    local[0].start()
     for i, (src, dst) in enumerate(
         [(rf_ref, ti.at[0]), (gf_ref, tf.at[0]), (rb_ref, ti.at[1]), (gb_ref, tf.at[1])]
     ):
@@ -140,8 +141,6 @@
         )
     loads.append(pltpu.make_async_copy(res_ref.at[0], res, ld.at[nch + 1]))
     loads.append(pltpu.make_async_copy(hb_ref.at[0], hb, ld.at[nch + 2]))
-    for load in loads:
-        load.start()
     for copy in local:
         copy.wait()
     packed = jnp.concatenate([ti[0].astype(F32), tf[0], ti[1].astype(F32), tf[1]], axis=1)
@@ -159,7 +158,7 @@
     zs = []
     for i in range(nag):
         zs.append(
-            send(remote(up_ref.at[0, part(i)], gbuf.at[c, p, part(i)],
+            send(remote(up.at[part(i)], gbuf.at[c, p, part(i)],
                         z_send.at[i], z_recv.at[i], section=below))
         )
     small = []
@@ -168,6 +167,9 @@
             send(remote(pack, tab.at[mine], sm_send.at[k - 1], sm_recv.at[k - 1],
                         expert=lax.rem(e + k, n)))
         )
+
+    for load in loads:
+        load.start()
 
     def expert_at(q):
         return 2 * q + c
@@ -393,6 +395,7 @@
         in_specs=[hbm] * 9,
         out_specs=(hbm, hbm, pl.BlockSpec(memory_space=pltpu.VMEM)),
         scratch_shapes=[
+            pltpu.VMEM((tokens, d), BF16),
             pltpu.VMEM((rows, ff), BF16),
             pltpu.VMEM((ff, d), BF16),
             pltpu.VMEM((tokens, d), BF16),
@@ -414,7 +417,7 @@
             pltpu.VMEM((tokens, d), BF16),
             pltpu.VMEM((rows, ff), BF16),
             dma((nch + 3,)),
-            dma((4,)),
+            dma((5,)),
             dma((n - 1,)),
             dma((n - 1,)),
             dma((nag,)),

time: 30.7 us -> 29.3 us (0.954)
  Pallas kernels: 29.9 us -> 28.5 us
    pallas_call x1, Pallas kernels: 27.8 us -> 26.4 us  [dense_body(): pl.pallas_call(functools.partial(kernel, n, sections, nch, nag, nbw), out...]
where the time goes in v3:
time: 29.3 us; the launch traced here: 29.2 us
  Pallas kernels  28.5 us (97%)
  between operations  0.64 us (2%)
    pallas_call x1, Pallas kernels, dense_body(): pl.pallas_call(functools.partial(kernel, n, sections, nch, nag, nbw), out...  26.4 us
    pallas_call x1, Pallas kernels, publish(): pl.pallas_call(publish_kernel, out_shape=tuple((jax.ShapeDtypeStruct(a.sh...  2.14 us

profile of v3, /device:TPU:0, one launch (start us, length us, event | category | flops | bytes accessed | tf_op | source)
XLA Modules:
  0.0 29.2 jit_solution(3613349927966500415)
XLA Ops:
  0.6 26.4 %shard_map.112 = (bf16[1,32,2048]{2,1,0:T(8,128)(2,1)}, bf16[1,256,1536]{2,1,0:T(8,128)(2,1)}, f32[1,256]{1,0:T(1,128)}) custom-call(bf16[1,256,1536]{2,1,0:T(8,128)(2,1)} %hf_ref.1, bf16[1,1536,2048]{2,1,0:T(8,128)(2,1)} %w_ref.1, bf16[1,32,2048]{2,1,0:T(8,128)(2,1)} %res_ref.1, s32[8,32]{1,0:T(8,128)} %bitcast.12, f32[8,32]{1,0:T(8,128)} %bitcast.13, ...), custom_call_target="tpu_custom_call" | custom-call | tf_op jit(solution)/shard_map/pallas_call | solution.py:388
  27.0 2.1 %shard_map.113 = (bf16[1,32,2048]{2,1,0:T(8,128)(2,1)}, bf16[1,256,1536]{2,1,0:T(8,128)(2,1)}, f32[1,256]{1,0:T(1,128)}) custom-call(bf16[1,32,2048]{2,1,0:T(8,128)(2,1)} %get-tuple-element.6.refs_0_, bf16[1,256,1536]{2,1,0:T(8,128)(2,1)} %get-tuple-element.7.refs_1_, f32[1,256]{1,0:T(1,128)} %get-tuple-element.8.refs_2_), custom_call_target="tpu_custom_call" | custom-call | tf_op jit(solution)/shard_map/pallas_call | solution.py:365
